TPU v7x, 256 devices: a whole 4x4x8 slice. The times are simulated.
256 devices in a mesh: leaf: 32 (over y, z), panel: 8 (over x, core).
Axes of the slice: x: 4, y: 4, z: 8, core: 2. Of those that a mesh axis runs over, the one named last changes fastest.
Arguments:
- child_front: float32 [32, 2, 8, 128, 2048], P('leaf', None, 'panel'), as said below
- parent_entries: float32 [32, 4, 8, 128, 512], P('leaf', None, 'panel'), as said below
- parent_of: int32 [32], replicated, may hold values from 0 to 31
- owner_slot: int32 [32], replicated, may hold values from 0 to 31, each once
- front_blocks: int32 [32], replicated, may hold values from 8 to 32, as said below
- block_lists: int32 [32, 8], replicated, may hold values from 0 to 31, as said below
Outputs:
- child_factor: float32 [32, 2, 8, 128, 1024], P('leaf', None, 'panel')
- parent_factor: float32 [32, 4, 8, 128, 512], P('leaf', None, 'panel')
Inputs may be any that keep to these rules, and one draw needn't show every extreme that they name: `front_blocks`: each entry is a multiple of the panel axis size; the largest equals 32. `block_lists`: the entries of a row are distinct, each below front_blocks of the child's parent, and entry k leaves the same remainder as k when divided by the panel axis size. `child_front`: symmetric, with a positive definite leading block of every front. `parent_entries`: the leading 512 rows form a symmetric positive definite block.
All inputs are finite; a program needn't handle non-finite values.
Results may differ from a plain program's by a relative error of at most 0.00044.
Values may be sent and summed in bfloat16 or wider, within the bound.
No kernel may reach another device: no remote copies, remote signals or barrier semaphores. Data moves between devices by JAX's collectives and lax.ppermute only.
A program may use at most 128 MiB of HBM per device.

v0:
```python
import jax
import jax.numpy as jnp
from jax import lax
from jax.sharding import PartitionSpec as P

BLK = 128
PANEL = 512
WC = 2048
PC = 1024
CBB = 8


def place_columns(block_rows, block_map):
    count_in = block_rows.shape[0]
    row_slots = block_rows.shape[1]
    pivot_blocks = PANEL // BLK
    onehot = (block_map[:, :, None] == jnp.arange(pivot_blocks)[None, None, :]).astype(jnp.bfloat16)
    split_blocks = block_rows.reshape(count_in, row_slots, BLK, CBB, BLK)
    placed = jnp.einsum(
        "muvkc,mkb->muvbc", split_blocks, onehot, preferred_element_type=jnp.float32
    )
    return placed.reshape(count_in, row_slots, BLK, PANEL)


def place_rows(assembled, placed, block_map, destination, panel_count, panel_index, leaf_index):
    count_in = placed.shape[0]
    row_slots = placed.shape[1]
    parent_slots = assembled.shape[0]
    grouped = block_map.reshape(count_in, row_slots, panel_count)
    pick = (jnp.arange(panel_count) == panel_index).astype(jnp.int32)
    row_blocks = jnp.sum(grouped * pick[None, None, :], axis=2)
    target = row_blocks[:, :, None] // panel_count == jnp.arange(parent_slots)[None, None, :]
    target = jnp.logical_and(target, (destination == leaf_index)[:, None, None]).astype(jnp.float32)
    return assembled + jnp.einsum("muvx,mut->tvx", placed, target, precision=lax.Precision.HIGHEST)


def on_device(child_front, parent_entries, parent_of, owner_slot, front_blocks, block_lists):
    panel_count = lax.axis_size("panel")
    panel_index = lax.axis_index("panel")
    leaf_index = lax.axis_index("leaf")
    row_slots = child_front.shape[1]
    parent_slots = parent_entries.shape[1]
    local_rows = child_front.reshape(row_slots * BLK, WC)
    factors = []
    for first_col in range(0, PC, PANEL):
        trailing = first_col + PANEL
        column = local_rows[:, first_col:trailing]
        gathered = lax.all_gather(
            column.reshape(row_slots, 1, BLK, PANEL), "panel", axis=1, tiled=True
        )
        gathered = gathered.reshape(WC, PANEL)
        pivot_block = jnp.linalg.cholesky(gathered[first_col:trailing])
        all_rows = jax.scipy.linalg.solve_triangular(pivot_block, gathered.T, lower=True).T
        all_rows = jnp.where(jnp.arange(WC)[:, None] >= first_col, all_rows, 0.0)
        own_rows = lax.dynamic_slice_in_dim(
            all_rows.reshape(row_slots, panel_count, BLK, PANEL), panel_index, 1, 1
        )
        own_rows = own_rows.reshape(row_slots * BLK, PANEL)
        update = jnp.dot(own_rows, all_rows[trailing:].T, precision=lax.Precision.HIGHEST)
        local_rows = jnp.concatenate(
            [local_rows[:, :trailing], local_rows[:, trailing:] - update], axis=1
        )
        factors.append(own_rows)
    child_factor = jnp.concatenate(factors, axis=1).reshape(1, row_slots, 1, BLK, PC)
    first_cb = PC // (BLK * panel_count)
    contribution = local_rows.reshape(row_slots, BLK, WC)[first_cb:, :, PC:].astype(jnp.bfloat16)
    parent_hits = (parent_of[:, None] == jnp.arange(owner_slot.shape[0])[None, :]).astype(jnp.int32)
    slot_of_child = jnp.sum(parent_hits * owner_slot[None, :], axis=1)
    live_mine = jnp.sum(jnp.where(owner_slot == leaf_index, front_blocks, 0))
    entries = parent_entries.reshape(parent_slots, BLK, PANEL)
    global_block = jnp.arange(parent_slots) * panel_count + panel_index
    initial = jnp.where((global_block < live_mine)[:, None, None], entries, 0.0)
    placed = place_columns(
        lax.all_gather(contribution[None], "leaf", axis=0, tiled=True), block_lists
    )
    assembled = place_rows(
        initial, placed, block_lists, slot_of_child, panel_count, panel_index, leaf_index
    )
    stacked = lax.all_gather(assembled[0], "panel", axis=0, tiled=True)
    pivot_block = jnp.linalg.cholesky(stacked[:PANEL])
    parent_rows = assembled.reshape(parent_slots * BLK, PANEL)
    parent_factor = jax.scipy.linalg.solve_triangular(pivot_block, parent_rows.T, lower=True).T
    return (child_factor, parent_factor.reshape(1, parent_slots, 1, BLK, PANEL))


def solution(mesh):
    in_specs = (
        P("leaf", None, "panel", None, None),
        P("leaf", None, "panel", None, None),
        P(),
        P(),
        P(),
        P(),
    )
    out_specs = (P("leaf", None, "panel", None, None), P("leaf", None, "panel", None, None))
    return jax.shard_map(
        on_device, mesh=mesh, in_specs=in_specs, out_specs=out_specs, check_vma=False
    )
```

profile of v0, /device:TPU:1, one launch (start us, length us, event | category | flops | bytes accessed | tf_op | source)
XLA Modules:
  0.0 736.7 jit_solution(10436099563935229929)
XLA Ops:
  9.2 40.2 %all-gather.7.cloned.1.call-done = f32[2,8,128,512]{3,2,0,1:T(8,128)} async-done(((f32[2,1,128,512]{3,2,0,1:T(8,128)}), f32[2,8,128,512]{3,2,0,1:T(8,128)}) %all-gather.7.cloned.1.call-update) | async-done | bytes 4194320 | tf_op jit(solution)/shard_map/all_gather | solution.py:48
  62.7 11.7 %cholesky.374 = f32[128,128]{1,0:T(8,128)S(1)} custom-call(f32[128,128]{1,0:T(8,128)S(1)} %cholesky.586), custom_call_target="Cholesky" | custom-call | tf_op jit(solution)/shard_map/jit(cholesky)/cholesky | solution.py:52
  74.5 9.8 %custom-call.35 = f32[1,128,128]{1,2,0:T(8,128)S(1)} custom-call(f32[1,128,128]{2,1,0:T(8,128)S(1)} %get-tuple-element.103), custom_call_target="InvertDiagBlocksLowerTriangular" | custom-call | tf_op jit(solution)/shard_map/jit(cholesky)/cholesky | solution.py:52
  85.1 11.9 %cholesky.393 = f32[128,128]{1,0:T(8,128)S(1)} custom-call(f32[128,128]{1,0:T(8,128)S(1)} %cholesky.590), custom_call_target="Cholesky" | custom-call | tf_op jit(solution)/shard_map/jit(cholesky)/cholesky | solution.py:52
  97.0 9.8 %custom-call.36 = f32[1,128,128]{1,2,0:T(8,128)S(1)} custom-call(f32[1,128,128]{2,1,0:T(8,128)S(1)} %get-tuple-element.100), custom_call_target="InvertDiagBlocksLowerTriangular" | custom-call | tf_op jit(solution)/shard_map/jit(cholesky)/cholesky | solution.py:52
  107.5 11.7 %cholesky.414 = f32[128,128]{1,0:T(8,128)S(1)} custom-call(f32[128,128]{1,0:T(8,128)S(1)} %cholesky.595), custom_call_target="Cholesky" | custom-call | tf_op jit(solution)/shard_map/jit(cholesky)/cholesky | solution.py:52
  119.9 9.8 %custom-call.37 = f32[1,128,128]{1,2,0:T(8,128)S(1)} custom-call(f32[1,128,128]{2,1,0:T(8,128)S(1)} %get-tuple-element.97), custom_call_target="InvertDiagBlocksLowerTriangular" | custom-call | tf_op jit(solution)/shard_map/jit(cholesky)/cholesky | solution.py:52
  130.3 12.1 %cholesky.431 = f32[128,128]{1,0:T(8,128)S(1)} custom-call(f32[128,128]{1,0:T(8,128)S(1)} %convolution_subtract_fusion.15), custom_call_target="Cholesky" | custom-call | tf_op jit(solution)/shard_map/jit(cholesky)/cholesky | solution.py:52
  154.5 39.3 %custom-call.38 = f32[4,128,128]{1,2,0:T(8,128)S(1)} custom-call(f32[4,128,128]{2,1,0:T(8,128)S(1)} %get-tuple-element.26), custom_call_target="InvertDiagBlocksLowerTriangular" | custom-call | tf_op jit(solution)/shard_map/jit(_solve_triangular)/triangular_solve | solution.py:53
  213.6 33.6 %all-gather.9.cloned.1.call-done = f32[2,8,128,512]{3,2,0,1:T(8,128)} async-done(((f32[2,1,128,512]{3,2,0,1:T(8,128)}), f32[2,8,128,512]{3,2,0,1:T(8,128)}) %all-gather.9.cloned.1.call-update) | async-done | bytes 4194320 | tf_op jit(solution)/shard_map/all_gather | solution.py:48
  263.9 11.7 %cholesky.446 = f32[128,128]{1,0:T(8,128)S(1)} custom-call(f32[128,128]{1,0:T(8,128)S(1)} %cholesky.599), custom_call_target="Cholesky" | custom-call | tf_op jit(solution)/shard_map/jit(cholesky)/cholesky | solution.py:52
  275.7 9.8 %custom-call.39 = f32[1,128,128]{1,2,0:T(8,128)S(1)} custom-call(f32[1,128,128]{2,1,0:T(8,128)S(1)} %get-tuple-element.93), custom_call_target="InvertDiagBlocksLowerTriangular" | custom-call | tf_op jit(solution)/shard_map/jit(cholesky)/cholesky | solution.py:52
  288.1 12.1 %cholesky.465 = f32[128,128]{1,0:T(8,128)S(1)} custom-call(f32[128,128]{1,0:T(8,128)S(1)} %cholesky.603), custom_call_target="Cholesky" | custom-call | tf_op jit(solution)/shard_map/jit(cholesky)/cholesky | solution.py:52
  301.5 9.8 %custom-call.40 = f32[1,128,128]{1,2,0:T(8,128)S(1)} custom-call(f32[1,128,128]{2,1,0:T(8,128)S(1)} %get-tuple-element.90), custom_call_target="InvertDiagBlocksLowerTriangular" | custom-call | tf_op jit(solution)/shard_map/jit(cholesky)/cholesky | solution.py:52
  312.9 11.7 %cholesky.486 = f32[128,128]{1,0:T(8,128)S(1)} custom-call(f32[128,128]{1,0:T(8,128)S(1)} %cholesky.608), custom_call_target="Cholesky" | custom-call | tf_op jit(solution)/shard_map/jit(cholesky)/cholesky | solution.py:52
  325.4 9.8 %custom-call.41 = f32[1,128,128]{1,2,0:T(8,128)S(1)} custom-call(f32[1,128,128]{2,1,0:T(8,128)S(1)} %get-tuple-element.87), custom_call_target="InvertDiagBlocksLowerTriangular" | custom-call | tf_op jit(solution)/shard_map/jit(cholesky)/cholesky | solution.py:52
  336.6 11.9 %cholesky.503 = f32[128,128]{1,0:T(8,128)S(1)} custom-call(f32[128,128]{1,0:T(8,128)S(1)} %convolution_subtract_fusion.14), custom_call_target="Cholesky" | custom-call | tf_op jit(solution)/shard_map/jit(cholesky)/cholesky | solution.py:52
  352.9 11.4 %while.7 = (s32[]{:T(128)}, f32[512,512]{1,0:T(8,128)}, s32[4,2]{0,1:T(2,128)S(1)}, f32[4,128,128]{2,1,0:T(8,128)S(1)}, s32[]{:T(128)}) while((s32[]{:T(128)}, f32[512,512]{1,0:T(8,128)}, s32[4,2]{0,1:T(2,128)S(1)}, f32[4,128,128]{2,1,0:T(8,128)S(1)}, s32[]{:T(128)}) %tuple.105), condition=%wide.while_cond.clone, body=%wide.while_body.clone.sunk | while | flops 2 | bytes 131181 | solution.py:53
  364.3 39.3 %custom-call.42 = f32[4,128,128]{1,2,0:T(8,128)S(1)} custom-call(f32[4,128,128]{2,1,0:T(8,128)S(1)} %get-tuple-element.27), custom_call_target="InvertDiagBlocksLowerTriangular" | custom-call | tf_op jit(solution)/shard_map/jit(_solve_triangular)/triangular_solve | solution.py:53
  425.7 94.6 %all-gather.11.cloned.1.call-done = bf16[32,128,1024]{2,1,0:T(8,128)(2,1)} async-done(((bf16[1,128,1024]{2,1,0:T(8,128)(2,1)}), bf16[32,128,1024]{2,1,0:T(8,128)(2,1)}) %all-gather.11.cloned.1.call-update) | async-done | bytes 8388624 | tf_op jit(solution)/shard_map/all_gather | solution.py:74
  529.1 8.9 %fusion.4 = f32[32,1,128,4,128]{4,3,2,0,1:T(4,128)} fusion(s32[32,8]{1,0:T(8,128)S(1)} %copy.54, bf16[32,128,8,128]{3,2,1,0:T(8,128)(2,1)} %bitcast.244), kind=kOutput, calls=%fused_computation.10 | convolution fusion | flops 33555456 | bytes 16778240 | tf_op jit(solution)/shard_map/muvkc,mkb->muvbc/dot_general | solution.py:19
  538.0 10.3 %reshape.264 = f32[32,128,512]{2,1,0:T(8,128)} reshape(f32[32,1,128,4,128]{4,3,2,0,1:T(4,128)} %fusion.4) | data formatting | bytes 16777216 | tf_op jit(solution)/shard_map/reshape.65
  548.2 10.4 %fusion.2 = f32[4,128,512]{2,0,1:T(4,128)S(1)} fusion(f32[32,128,512]{2,1,0:T(8,128)} %reshape.264, s32[32]{0:T(128)S(1)} %get-tuple-element.112, pred[32]{0:T(512)(128)(4,1)S(1)} %broadcast_compare_fusion), kind=kOutput, calls=%fused_computation.8 | convolution fusion | flops 100663552 | bytes 9437344 | tf_op jit(solution)/shard_map/muvx,mut->tvx/dot_general | solution.py:34
  565.5 24.5 %all-gather.13.cloned.1.call-done = f32[1,1024,512]{1,2,0:T(8,128)} async-done(((f32[1,128,512]{1,2,0:T(8,128)}), f32[1,1024,512]{1,2,0:T(8,128)}) %all-gather.13.cloned.1.call-update) | async-done | bytes 2097168 | tf_op jit(solution)/shard_map/all_gather | solution.py:79
  593.1 11.7 %cholesky.518 = f32[128,128]{1,0:T(8,128)S(1)} custom-call(f32[128,128]{1,0:T(8,128)S(1)} %cholesky.612), custom_call_target="Cholesky" | custom-call | tf_op jit(solution)/shard_map/jit(cholesky)/cholesky | solution.py:80
  605.0 9.8 %custom-call.43 = f32[1,128,128]{1,2,0:T(8,128)S(1)} custom-call(f32[1,128,128]{2,1,0:T(8,128)S(1)} %get-tuple-element.83), custom_call_target="InvertDiagBlocksLowerTriangular" | custom-call | tf_op jit(solution)/shard_map/jit(cholesky)/cholesky | solution.py:80
  615.5 11.7 %cholesky.537 = f32[128,128]{1,0:T(8,128)S(1)} custom-call(f32[128,128]{1,0:T(8,128)S(1)} %cholesky.616), custom_call_target="Cholesky" | custom-call | tf_op jit(solution)/shard_map/jit(cholesky)/cholesky | solution.py:80
  628.6 10.0 %custom-call.44 = f32[1,128,128]{1,2,0:T(8,128)S(1)} custom-call(f32[1,128,128]{2,1,0:T(8,128)S(1)} %get-tuple-element.80), custom_call_target="InvertDiagBlocksLowerTriangular" | custom-call | tf_op jit(solution)/shard_map/jit(cholesky)/cholesky | solution.py:80
  639.2 11.7 %cholesky.558 = f32[128,128]{1,0:T(8,128)S(1)} custom-call(f32[128,128]{1,0:T(8,128)S(1)} %cholesky.621), custom_call_target="Cholesky" | custom-call | tf_op jit(solution)/shard_map/jit(cholesky)/cholesky | solution.py:80
  651.6 9.8 %custom-call.45 = f32[1,128,128]{1,2,0:T(8,128)S(1)} custom-call(f32[1,128,128]{2,1,0:T(8,128)S(1)} %get-tuple-element.77), custom_call_target="InvertDiagBlocksLowerTriangular" | custom-call | tf_op jit(solution)/shard_map/jit(cholesky)/cholesky | solution.py:80
  662.0 11.9 %cholesky.575 = f32[128,128]{1,0:T(8,128)S(1)} custom-call(f32[128,128]{1,0:T(8,128)S(1)} %convolution_subtract_fusion.13), custom_call_target="Cholesky" | custom-call | tf_op jit(solution)/shard_map/jit(cholesky)/cholesky | solution.py:80
  685.9 39.3 %custom-call.27 = f32[4,128,128]{1,2,0:T(8,128)S(1)} custom-call(f32[4,128,128]{2,1,0:T(8,128)S(1)} %get-tuple-element.19), custom_call_target="InvertDiagBlocksLowerTriangular" | custom-call | tf_op jit(solution)/shard_map/jit(_solve_triangular)/triangular_solve | solution.py:82
  (200 shorter events, 159.4 us)
Async XLA Ops:
  7.2 42.2 %all-gather.7.cloned.1.call-start = ((), (), s32[]{:S(2)}) async-start(), calls=%async_computation | async-start | bytes 4718592 | tf_op jit(solution)/shard_map/all_gather | solution.py:48
  9.1 238.2 %all-gather.9.cloned.1.call-start = ((), (), s32[]{:S(2)}) async-start(), calls=%async_computation.1 | async-start | bytes 4718592 | tf_op jit(solution)/shard_map/all_gather | solution.py:48
  58.9 1.9 copy-start
  193.8 5.7 copy-start.1
  206.0 1.6 copy-start.8
  207.4 5.1 copy-start.4
  212.5 307.8 %all-gather.11.cloned.1.call-start = ((), (), s32[]{:S(2)}) async-start(), calls=%async_computation.2 | async-start | bytes 8650752 | tf_op jit(solution)/shard_map/all_gather | solution.py:74
  256.9 1.9 copy-start.2
  262.9 1.0 copy-start.7
  403.6 5.8 copy-start.3
  418.8 2.4 copy-start.6
  418.9 3.7 copy-start.9
  419.2 5.0 copy-start.10
  419.2 5.0 copy-start.11
  419.3 6.3 copy-start.12
  422.5 167.6 %all-gather.13.cloned.1.call-start = ((), (), s32[]{:S(2)}) async-start(), calls=%async_computation.3 | async-start | bytes 2359296 | tf_op jit(solution)/shard_map/all_gather | solution.py:79
  558.7 3.5 copy-start.5
Sparse Core Ops, SparseCore 0:
  10.4 38.8 all-gather.6
  212.6 34.6 all-gather.8
  422.6 97.6 all-gather.10
  562.3 27.6 all-gather.12
where the time goes:
time: 747 us; the launch traced here: 737 us
  other arithmetic  369 us (49%)
  waiting for transfers between devices  193 us (26%)
  local copies, waits for them, and re-layouts  90.3 us (12%)
  matrix products  61.6 us (8%)
  between operations  22.8 us (3%)
    another operation x29, other arithmetic, on_device(): pivot_block = jnp.linalg.cholesky(gathered[first_col:trailing])  159 us
    all_gather x1, waiting for transfers between devices, on_device(): lax.all_gather(contribution[None], 'leaf', axis=0, tiled=True)  94.6 us
    another operation x5, other arithmetic, on_device(): jax.scipy.linalg.solve_triangular(pivot_block, gathered.T, lower=True)  79.9 us
    another operation x15, other arithmetic, on_device(): pivot_block = jnp.linalg.cholesky(stacked[:PANEL])  79.4 us
    all_gather x2, waiting for transfers between devices, on_device(): lax.all_gather(column.reshape(row_slots, 1, BLK, PANEL), 'panel', axis=1,...  73.8 us
    another operation x2, other arithmetic, on_device(): jax.scipy.linalg.solve_triangular(pivot_block, parent_rows.T, lower=True)  39.4 us
    unnamed x34, local copies, waits for them, and re-layouts  27 us
    all_gather x1, waiting for transfers between devices, on_device(): stacked = lax.all_gather(assembled[0], 'panel', axis=0, tiled=True)  24.5 us
  transfers between devices with their start and end apart: 4, of which 4 were waited for; matrix products, arithmetic and copies ran while one was open for 1% of the time, Pallas kernels for 0%

commit v1 on v0

--- a/solution.py
+++ b/solution.py
@@ -45,9 +45,23 @@
     for first_col in range(0, PC, PANEL):
         trailing = first_col + PANEL
         column = local_rows[:, first_col:trailing]
-        gathered = lax.all_gather(
-            column.reshape(row_slots, 1, BLK, PANEL), "panel", axis=1, tiled=True
-        )
+        x = column.reshape(row_slots, 1, BLK, PANEL)
+        ways, here, step = (lax.axis_size("panel"), lax.axis_index("panel"), x.shape[1])
+        dims = [n * ways if d == 1 else n for d, n in enumerate(x.shape)]
+        gathered = lax.dynamic_update_slice_in_dim(jnp.zeros(dims, x.dtype), x, here * step, axis=1)
+        going_up = going_down = x
+        for far in range(1, ways // 2 + 1):
+            going_up = lax.ppermute(going_up, "panel", [(d, (d + 1) % ways) for d in range(ways)])
+            gathered = lax.dynamic_update_slice_in_dim(
+                gathered, going_up, (here - far) % ways * step, axis=1
+            )
+            if 2 * far < ways:
+                going_down = lax.ppermute(
+                    going_down, "panel", [(d, (d - 1) % ways) for d in range(ways)]
+                )
+                gathered = lax.dynamic_update_slice_in_dim(
+                    gathered, going_down, (here + far) % ways * step, axis=1
+                )
         gathered = gathered.reshape(WC, PANEL)
         pivot_block = jnp.linalg.cholesky(gathered[first_col:trailing])
         all_rows = jax.scipy.linalg.solve_triangular(pivot_block, gathered.T, lower=True).T

time: 747 us -> 961 us (1.29)
  local copies, waits for them, and re-layouts: 90.3 us -> 316 us
  waiting for transfers between devices: 193 us -> 146 us
  starting transfers between devices: 0.16 us -> 36.1 us
    dynamic_update_slice x0 -> x16, local copies, waits for them, and re-layouts: none -> 233 us  [the longest x8 117 us: on_device(): lax.dynamic_update_slice_in_dim(gathered, going_up, (here - far) % ways *...]
    all_gather x2 -> x0, waiting for transfers between devices: 73.8 us -> none  [on_device(): lax.all_gather(column.reshape(row_slots, 1, BLK, PANEL), 'panel', axis=1,...]
    ppermute x0 -> x14, starting transfers between devices: none -> 36 us  [the longest x6 21.2 us: on_device(): lax.ppermute(going_down, 'panel', [(d, (d - 1) % ways) for d in range(way...]
    ppermute x0 -> x14, waiting for transfers between devices: none -> 18.4 us  [the longest x8 16.8 us: on_device(): lax.ppermute(going_up, 'panel', [(d, (d + 1) % ways) for d in range(ways)])]
    all_gather x2 -> x0, local copies, waits for them, and re-layouts: 10.9 us -> none  [on_device(): lax.all_gather(column.reshape(row_slots, 1, BLK, PANEL), 'panel', axis=1,...]
    another operation x13 -> x15, local copies, waits for them, and re-layouts: 18.7 us -> 23.1 us
    unnamed x34 -> x36, local copies, waits for them, and re-layouts: 27 us -> 27 us
  transfers between devices with their start and end apart: 4 -> 16, of which waited for: 4 -> 12; matrix products, arithmetic and copies ran while one was open for 1% -> 23% of each run, Pallas kernels for 0% -> 0%
where the time goes in v1:
time: 961 us; the launch traced here: 950 us
  other arithmetic  369 us (38%)
  local copies, waits for them, and re-layouts  316 us (33%)
  waiting for transfers between devices  146 us (15%)
  matrix products  60 us (6%)
  starting transfers between devices  36.1 us (4%)
  between operations  22.9 us (2%)
    another operation x29, other arithmetic, on_device(): pivot_block = jnp.linalg.cholesky(gathered[first_col:trailing])  159 us
    dynamic_update_slice x8, local copies, waits for them, and re-layouts, on_device(): lax.dynamic_update_slice_in_dim(gathered, going_up, (here - far) % ways *...  117 us
    all_gather x1, waiting for transfers between devices, on_device(): lax.all_gather(contribution[None], 'leaf', axis=0, tiled=True)  103 us
    dynamic_update_slice x6, local copies, waits for them, and re-layouts, on_device(): lax.dynamic_update_slice_in_dim(gathered, going_down, (here + far) % ways...  87.2 us
    another operation x5, other arithmetic, on_device(): jax.scipy.linalg.solve_triangular(pivot_block, gathered.T, lower=True)  79.9 us
    another operation x15, other arithmetic, on_device(): pivot_block = jnp.linalg.cholesky(stacked[:PANEL])  79.4 us
    another operation x2, other arithmetic, on_device(): jax.scipy.linalg.solve_triangular(pivot_block, parent_rows.T, lower=True)  39.4 us
    dynamic_update_slice x2, local copies, waits for them, and re-layouts, on_device(): lax.dynamic_update_slice_in_dim(jnp.zeros(dims, x.dtype), x, here * step,...  29.1 us
  transfers between devices with their start and end apart: 16, of which 12 were waited for; matrix products, arithmetic and copies ran while one was open for 23% of the time, Pallas kernels for 0%

profile of v1, /device:TPU:1, one launch (start us, length us, event | category | flops | bytes accessed | tf_op | source)
XLA Modules:
  0.0 950.3 jit_solution(12834793237489840405)
XLA Ops:
  39.3 14.5 %dynamic_update_slice.48 = f32[2,8,128,512]{2,1,0,3:T(8,128)} dynamic-update-slice(f32[2,8,128,512]{2,1,0,3:T(8,128)} %broadcast.285.clone, f32[2,1,128,512]{2,1,0,3:T(1,128)S(1)} %copy.59, s32[]{:T(128)} %copy.165, s32[]{:T(128)S(6)} %select_n.108, s32[]{:T(128)} %copy.165, s32[]{:T(128)} %copy.165) | dynamic-update-slice | bytes 1048580 | tf_op jit(solution)/shard_map/dynamic_update_slice | solution.py:51
  53.8 14.5 %dynamic_update_slice.49 = f32[2,8,128,512]{2,1,0,3:T(8,128)} dynamic-update-slice(f32[2,8,128,512]{2,1,0,3:T(8,128)} %dynamic_update_slice.48, f32[2,1,128,512]{2,1,0,3:T(1,128)S(1)} %collective-permute-done, s32[]{:T(128)} %copy.165, s32[]{:T(128)S(6)} %select_n.110, s32[]{:T(128)} %copy.165, s32[]{:T(128)} %copy.165) | dynamic-update-slice | bytes 1048580 | tf_op jit(solution)/shard_map/dynamic_update_slice | solution.py:55
  68.4 14.5 %dynamic_update_slice.50 = f32[2,8,128,512]{2,1,0,3:T(8,128)} dynamic-update-slice(f32[2,8,128,512]{2,1,0,3:T(8,128)} %dynamic_update_slice.49, f32[2,1,128,512]{2,1,0,3:T(1,128)S(1)} %collective-permute-done.1, s32[]{:T(128)} %copy.165, s32[]{:T(128)S(6)} %select_n.112, s32[]{:T(128)} %copy.165, s32[]{:T(128)} %copy.165) | dynamic-update-slice | bytes 1048580 | tf_op jit(solution)/shard_map/dynamic_update_slice | solution.py:62
  82.9 14.5 %dynamic_update_slice.51 = f32[2,8,128,512]{2,1,0,3:T(8,128)} dynamic-update-slice(f32[2,8,128,512]{2,1,0,3:T(8,128)} %dynamic_update_slice.50, f32[2,1,128,512]{2,1,0,3:T(1,128)S(1)} %collective-permute-done.2, s32[]{:T(128)} %copy.165, s32[]{:T(128)S(6)} %select_n.114, s32[]{:T(128)} %copy.165, s32[]{:T(128)} %copy.165) | dynamic-update-slice | bytes 1048580 | tf_op jit(solution)/shard_map/dynamic_update_slice | solution.py:55
  97.4 14.5 %dynamic_update_slice.52 = f32[2,8,128,512]{2,1,0,3:T(8,128)} dynamic-update-slice(f32[2,8,128,512]{2,1,0,3:T(8,128)} %dynamic_update_slice.51, f32[2,1,128,512]{2,1,0,3:T(1,128)S(1)} %collective-permute-done.3, s32[]{:T(128)} %copy.165, s32[]{:T(128)S(6)} %select_n.116, s32[]{:T(128)} %copy.165, s32[]{:T(128)} %copy.165) | dynamic-update-slice | bytes 1048580 | tf_op jit(solution)/shard_map/dynamic_update_slice | solution.py:62
  111.9 14.5 %dynamic_update_slice.53 = f32[2,8,128,512]{2,1,0,3:T(8,128)} dynamic-update-slice(f32[2,8,128,512]{2,1,0,3:T(8,128)} %dynamic_update_slice.52, f32[2,1,128,512]{2,1,0,3:T(1,128)S(1)} %collective-permute-done.4, s32[]{:T(128)} %copy.165, s32[]{:T(128)S(6)} %select_n.118, s32[]{:T(128)} %copy.165, s32[]{:T(128)} %copy.165) | dynamic-update-slice | bytes 1048580 | tf_op jit(solution)/shard_map/dynamic_update_slice | solution.py:55
  126.5 14.5 %dynamic_update_slice.54 = f32[2,8,128,512]{2,1,0,3:T(8,128)} dynamic-update-slice(f32[2,8,128,512]{2,1,0,3:T(8,128)} %dynamic_update_slice.53, f32[2,1,128,512]{2,1,0,3:T(1,128)} %collective-permute-done.5, s32[]{:T(128)} %copy.165, s32[]{:T(128)S(6)} %select_n.120, s32[]{:T(128)} %copy.165, s32[]{:T(128)} %copy.165) | dynamic-update-slice | bytes 1048580 | tf_op jit(solution)/shard_map/dynamic_update_slice | solution.py:62
  141.0 15.0 %dynamic_update_slice.55 = f32[2,8,128,512]{2,1,0,3:T(8,128)} dynamic-update-slice(f32[2,8,128,512]{2,1,0,3:T(8,128)} %dynamic_update_slice.54, f32[2,1,128,512]{2,1,0,3:T(1,128)} %collective-permute-done.6, s32[]{:T(128)} %copy.165, s32[]{:T(128)S(6)} %select_n.122, s32[]{:T(128)} %copy.165, s32[]{:T(128)} %copy.165) | dynamic-update-slice | bytes 1048580 | tf_op jit(solution)/shard_map/dynamic_update_slice | solution.py:55
  164.0 11.7 %cholesky.374 = f32[128,128]{1,0:T(8,128)S(1)} custom-call(f32[128,128]{1,0:T(8,128)S(1)} %cholesky.586), custom_call_target="Cholesky" | custom-call | tf_op jit(solution)/shard_map/jit(cholesky)/cholesky | solution.py:66
  186.4 11.9 %cholesky.393 = f32[128,128]{1,0:T(8,128)S(1)} custom-call(f32[128,128]{1,0:T(8,128)S(1)} %cholesky.590), custom_call_target="Cholesky" | custom-call | tf_op jit(solution)/shard_map/jit(cholesky)/cholesky | solution.py:66
  208.8 11.7 %cholesky.414 = f32[128,128]{1,0:T(8,128)S(1)} custom-call(f32[128,128]{1,0:T(8,128)S(1)} %cholesky.595), custom_call_target="Cholesky" | custom-call | tf_op jit(solution)/shard_map/jit(cholesky)/cholesky | solution.py:66
  231.6 12.1 %cholesky.431 = f32[128,128]{1,0:T(8,128)S(1)} custom-call(f32[128,128]{1,0:T(8,128)S(1)} %convolution_subtract_fusion.11), custom_call_target="Cholesky" | custom-call | tf_op jit(solution)/shard_map/jit(cholesky)/cholesky | solution.py:66
  255.8 39.3 %custom-call.38 = f32[4,128,128]{1,2,0:T(8,128)S(1)} custom-call(f32[4,128,128]{2,1,0:T(8,128)S(1)} %get-tuple-element.26), custom_call_target="InvertDiagBlocksLowerTriangular" | custom-call | tf_op jit(solution)/shard_map/jit(_solve_triangular)/triangular_solve | solution.py:67
  341.4 14.5 %dynamic_update_slice.56 = f32[2,8,128,512]{2,1,0,3:T(8,128)} dynamic-update-slice(f32[2,8,128,512]{2,1,0,3:T(8,128)} %broadcast.285, f32[2,1,128,512]{2,1,0,3:T(1,128)S(1)} %copy.64, s32[]{:T(128)} %copy.165, s32[]{:T(128)S(6)} %select_n.108, s32[]{:T(128)} %copy.165, s32[]{:T(128)} %copy.165) | dynamic-update-slice | bytes 1048580 | tf_op jit(solution)/shard_map/dynamic_update_slice | solution.py:51
  356.0 14.5 %dynamic_update_slice.57 = f32[2,8,128,512]{2,1,0,3:T(8,128)} dynamic-update-slice(f32[2,8,128,512]{2,1,0,3:T(8,128)} %dynamic_update_slice.56, f32[2,1,128,512]{2,1,0,3:T(1,128)S(1)} %collective-permute-done.7, s32[]{:T(128)} %copy.165, s32[]{:T(128)S(6)} %select_n.110, s32[]{:T(128)} %copy.165, s32[]{:T(128)} %copy.165) | dynamic-update-slice | bytes 1048580 | tf_op jit(solution)/shard_map/dynamic_update_slice | solution.py:55
  370.5 14.5 %dynamic_update_slice.58 = f32[2,8,128,512]{2,1,0,3:T(8,128)} dynamic-update-slice(f32[2,8,128,512]{2,1,0,3:T(8,128)} %dynamic_update_slice.57, f32[2,1,128,512]{2,1,0,3:T(1,128)S(1)} %collective-permute-done.8, s32[]{:T(128)} %copy.165, s32[]{:T(128)S(6)} %select_n.112, s32[]{:T(128)} %copy.165, s32[]{:T(128)} %copy.165) | dynamic-update-slice | bytes 1048580 | tf_op jit(solution)/shard_map/dynamic_update_slice | solution.py:62
  385.0 14.5 %dynamic_update_slice.59 = f32[2,8,128,512]{2,1,0,3:T(8,128)} dynamic-update-slice(f32[2,8,128,512]{2,1,0,3:T(8,128)} %dynamic_update_slice.58, f32[2,1,128,512]{2,1,0,3:T(1,128)} %copy-done.9, s32[]{:T(128)} %copy.165, s32[]{:T(128)S(6)} %select_n.114, s32[]{:T(128)} %copy.165, s32[]{:T(128)} %copy.165) | dynamic-update-slice | bytes 1048580 | tf_op jit(solution)/shard_map/dynamic_update_slice | solution.py:55
  399.6 14.5 %dynamic_update_slice.60 = f32[2,8,128,512]{2,1,0,3:T(8,128)} dynamic-update-slice(f32[2,8,128,512]{2,1,0,3:T(8,128)} %dynamic_update_slice.59, f32[2,1,128,512]{2,1,0,3:T(1,128)} %collective-permute-done.10, s32[]{:T(128)} %copy.165, s32[]{:T(128)S(6)} %select_n.116, s32[]{:T(128)} %copy.165, s32[]{:T(128)} %copy.165) | dynamic-update-slice | bytes 1048580 | tf_op jit(solution)/shard_map/dynamic_update_slice | solution.py:62
  414.1 14.5 %dynamic_update_slice.61 = f32[2,8,128,512]{2,1,0,3:T(8,128)} dynamic-update-slice(f32[2,8,128,512]{2,1,0,3:T(8,128)} %dynamic_update_slice.60, f32[2,1,128,512]{2,1,0,3:T(1,128)} %collective-permute-done.11, s32[]{:T(128)} %copy.165, s32[]{:T(128)S(6)} %select_n.118, s32[]{:T(128)} %copy.165, s32[]{:T(128)} %copy.165) | dynamic-update-slice | bytes 1048580 | tf_op jit(solution)/shard_map/dynamic_update_slice | solution.py:55
  428.6 14.5 %dynamic_update_slice.62 = f32[2,8,128,512]{2,1,0,3:T(8,128)} dynamic-update-slice(f32[2,8,128,512]{2,1,0,3:T(8,128)} %dynamic_update_slice.61, f32[2,1,128,512]{2,1,0,3:T(1,128)} %collective-permute-done.12, s32[]{:T(128)} %copy.165, s32[]{:T(128)S(6)} %select_n.120, s32[]{:T(128)} %copy.165, s32[]{:T(128)} %copy.165) | dynamic-update-slice | bytes 1048580 | tf_op jit(solution)/shard_map/dynamic_update_slice | solution.py:62
  443.2 14.5 %dynamic_update_slice.63 = f32[2,8,128,512]{2,1,0,3:T(8,128)} dynamic-update-slice(f32[2,8,128,512]{2,1,0,3:T(8,128)} %dynamic_update_slice.62, f32[2,1,128,512]{2,1,0,3:T(1,128)} %collective-permute-done.13, s32[]{:T(128)} %copy.165, s32[]{:T(128)S(6)} %select_n.122, s32[]{:T(128)} %copy.165, s32[]{:T(128)} %copy.165) | dynamic-update-slice | bytes 1048580 | tf_op jit(solution)/shard_map/dynamic_update_slice | solution.py:55
  468.8 11.7 %cholesky.446 = f32[128,128]{1,0:T(8,128)S(1)} custom-call(f32[128,128]{1,0:T(8,128)S(1)} %cholesky.599), custom_call_target="Cholesky" | custom-call | tf_op jit(solution)/shard_map/jit(cholesky)/cholesky | solution.py:66
  493.1 12.1 %cholesky.465 = f32[128,128]{1,0:T(8,128)S(1)} custom-call(f32[128,128]{1,0:T(8,128)S(1)} %cholesky.603), custom_call_target="Cholesky" | custom-call | tf_op jit(solution)/shard_map/jit(cholesky)/cholesky | solution.py:66
  517.9 11.7 %cholesky.486 = f32[128,128]{1,0:T(8,128)S(1)} custom-call(f32[128,128]{1,0:T(8,128)S(1)} %cholesky.608), custom_call_target="Cholesky" | custom-call | tf_op jit(solution)/shard_map/jit(cholesky)/cholesky | solution.py:66
  541.6 11.9 %cholesky.503 = f32[128,128]{1,0:T(8,128)S(1)} custom-call(f32[128,128]{1,0:T(8,128)S(1)} %convolution_subtract_fusion.10), custom_call_target="Cholesky" | custom-call | tf_op jit(solution)/shard_map/jit(cholesky)/cholesky | solution.py:66
  569.3 39.3 %custom-call.42 = f32[4,128,128]{1,2,0:T(8,128)S(1)} custom-call(f32[4,128,128]{2,1,0:T(8,128)S(1)} %get-tuple-element.27), custom_call_target="InvertDiagBlocksLowerTriangular" | custom-call | tf_op jit(solution)/shard_map/jit(_solve_triangular)/triangular_solve | solution.py:67
  630.3 103.4 %all-gather.5.cloned.1.call-done = bf16[32,128,1024]{2,1,0:T(8,128)(2,1)} async-done(((bf16[1,128,1024]{2,1,0:T(8,128)(2,1)}), bf16[32,128,1024]{2,1,0:T(8,128)(2,1)}) %all-gather.5.cloned.1.call-update) | async-done | bytes 8388624 | tf_op jit(solution)/shard_map/all_gather | solution.py:88
  778.9 24.5 %all-gather.7.cloned.1.call-done = f32[1,1024,512]{1,2,0:T(8,128)} async-done(((f32[1,128,512]{1,2,0:T(8,128)}), f32[1,1024,512]{1,2,0:T(8,128)}) %all-gather.7.cloned.1.call-update) | async-done | bytes 2097168 | tf_op jit(solution)/shard_map/all_gather | solution.py:93
  806.6 11.7 %cholesky.518 = f32[128,128]{1,0:T(8,128)S(1)} custom-call(f32[128,128]{1,0:T(8,128)S(1)} %cholesky.612), custom_call_target="Cholesky" | custom-call | tf_op jit(solution)/shard_map/jit(cholesky)/cholesky | solution.py:94
  828.9 11.7 %cholesky.537 = f32[128,128]{1,0:T(8,128)S(1)} custom-call(f32[128,128]{1,0:T(8,128)S(1)} %cholesky.616), custom_call_target="Cholesky" | custom-call | tf_op jit(solution)/shard_map/jit(cholesky)/cholesky | solution.py:94
  875.5 11.9 %cholesky.575 = f32[128,128]{1,0:T(8,128)S(1)} custom-call(f32[128,128]{1,0:T(8,128)S(1)} %convolution_subtract_fusion.9), custom_call_target="Cholesky" | custom-call | tf_op jit(solution)/shard_map/jit(cholesky)/cholesky | solution.py:94
  899.3 39.3 %custom-call.27 = f32[4,128,128]{1,2,0:T(8,128)S(1)} custom-call(f32[4,128,128]{2,1,0:T(8,128)S(1)} %get-tuple-element.19), custom_call_target="InvertDiagBlocksLowerTriangular" | custom-call | tf_op jit(solution)/shard_map/jit(_solve_triangular)/triangular_solve | solution.py:96
  (242 shorter events, 345.8 us)
Async XLA Ops:
  7.2 726.6 %all-gather.5.cloned.1.call-start = ((), (), s32[]{:S(2)}) async-start(), calls=%async_computation | async-start | bytes 8650752 | tf_op jit(solution)/shard_map/all_gather | solution.py:88
  8.7 8.7 collective-permute-start
  11.3 8.9 collective-permute-start.1
  17.4 8.6 collective-permute-start.2
  20.2 8.9 collective-permute-start.3
  26.0 8.6 collective-permute-start.4
  29.1 97.4 %collective-permute-start.5 = (f32[2,1,128,512]{2,1,0,3:T(1,128)S(1)}, f32[2,1,128,512]{2,1,0,3:T(1,128)}, u32[]{:S(2)}, u32[]{:S(2)}) collective-permute-start(f32[2,1,128,512]{2,1,0,3:T(1,128)S(1)} %collective-permute-done.3), channel_id=1, source_target_pairs={{0,7},{1,0},{2,1},{3,2},{4,3},{5,4},{6,5},{7,6},{8,15},{9,8},{10,9... | collective-permute-start | bytes 1572872 | tf_op jit(solution)/shard_map/ppermute | solution.py:59
  34.6 106.4 %collective-permute-start.6 = (f32[2,1,128,512]{2,1,0,3:T(1,128)S(1)}, f32[2,1,128,512]{2,1,0,3:T(1,128)}, u32[]{:S(2)}, u32[]{:S(2)}) collective-permute-start(f32[2,1,128,512]{2,1,0,3:T(1,128)S(1)} %collective-permute-done.4), channel_id=1, source_target_pairs={{0,1},{1,2},{2,3},{3,4},{4,5},{5,6},{6,7},{7,0},{8,9},{9,10},{10,1... | collective-permute-start | bytes 1572872 | tf_op jit(solution)/shard_map/ppermute | solution.py:54
  160.2 1.9 copy-start
  295.1 3.4 copy-start.1
  306.1 1.6 copy-start.8
  307.5 4.3 copy-start.4
  312.2 6.1 collective-permute-start.7
  312.2 8.9 collective-permute-start.8
  318.3 9.4 collective-permute-start.9
  321.1 8.7 collective-permute-start.10
  327.7 2.1 copy-start.9
  327.7 9.9 %collective-permute-start.11 = (f32[2,1,128,512]{2,1,0,3:T(1,128)S(1)}, f32[2,1,128,512]{2,1,0,3:T(1,128)}, u32[]{:S(2)}, u32[]{:S(2)}) collective-permute-start(f32[2,1,128,512]{2,1,0,3:T(1,128)S(1)} %collective-permute-done.9), channel_id=1, source_target_pairs={{0,1},{1,2},{2,3},{3,4},{4,5},{5,6},{6,7},{7,0},{8,9},{9,10},{10,1... | collective-permute-start | bytes 1572872 | tf_op jit(solution)/shard_map/ppermute | solution.py:54
  329.8 98.8 %collective-permute-start.12 = (f32[2,1,128,512]{2,1,0,3:T(1,128)}, f32[2,1,128,512]{2,1,0,3:T(1,128)}, u32[]{:S(2)}, u32[]{:S(2)}) collective-permute-start(f32[2,1,128,512]{2,1,0,3:T(1,128)} %collective-permute-done.10), channel_id=1, source_target_pairs={{0,7},{1,0},{2,1},{3,2},{4,3},{5,4},{6,5},{7,6},{8,15},{9,8},{10,9... | collective-permute-start | bytes 1572872 | tf_op jit(solution)/shard_map/ppermute | solution.py:59
  337.7 105.5 %collective-permute-start.13 = (f32[2,1,128,512]{2,1,0,3:T(1,128)}, f32[2,1,128,512]{2,1,0,3:T(1,128)}, u32[]{:S(2)}, u32[]{:S(2)}) collective-permute-start(f32[2,1,128,512]{2,1,0,3:T(1,128)} %collective-permute-done.11), channel_id=1, source_target_pairs={{0,1},{1,2},{2,3},{3,4},{4,5},{5,6},{6,7},{7,0},{8,9},{9,10},{10,1... | collective-permute-start | bytes 1572872 | tf_op jit(solution)/shard_map/ppermute | solution.py:54
  461.9 1.9 copy-start.2
  467.9 1.0 copy-start.7
  608.6 4.3 copy-start.3
  623.4 2.4 copy-start.6
  623.4 3.7 copy-start.10
  623.8 5.0 copy-start.11
  623.8 5.0 copy-start.12
  623.8 6.3 copy-start.13
  627.0 176.4 %all-gather.7.cloned.1.call-start = ((), (), s32[]{:S(2)}) async-start(), calls=%async_computation.1 | async-start | bytes 2359296 | tf_op jit(solution)/shard_map/all_gather | solution.py:93
  772.1 3.5 copy-start.5
Sparse Core Ops, SparseCore 0:
  627.2 106.5 all-gather.4
  775.8 27.6 all-gather.6
